TPU v7x, 32 devices: a whole 2x2x4 slice. The times are simulated.
32 devices in a mesh: grp: 16 (over z, x, core), mem: 2 (over y).
Axes of the slice: x: 2, y: 2, z: 4, core: 2. Of those that a mesh axis runs over, the one named last changes fastest.
Arguments:
- forcing: float32 [16, 256, 32, 128], P(None, 'grp', 'mem'), may hold values from -8 to 8
- aggregate: int32 [64, 8, 32], P('grp', 'mem'), may hold values from 0 to 8191, as said below
- factors: float32 [64, 128, 128], P('mem'), may hold values from -1.5 to 1.5, as said below
Outputs:
- solution: float32 [16, 256, 32, 128], P(None, 'grp', 'mem')
Inputs may be any that keep to these rules, and one draw needn't show every extreme that they name: Coarse unknowns are numbered over the fine blocks with the first block index taken modulo half the number of blocks along the first dimension, consecutive numbers lying close together in the other dimensions, so that an aggregate joins blocks of both halves of the grid; a few blocks take the entry of a block beside them. `factors`: each of the 64 blocks is lower triangular with its diagonal between 0.5 and 1.5.
All inputs are finite; a program needn't handle non-finite values.
Results may differ from a plain program's by a relative error of at most 0.00013.
Values sent between devices are 32-bit elements; how exact they have to be, the bound alone decides.
A program may use at most 128 MiB of HBM per device.

v0:
```python
import jax
import jax.numpy as jnp
from jax import lax
from jax.sharding import PartitionSpec as P

NC = 8192
PRE = 3
POST = 2
relaxation = 0.8


def with_halo(cells, sides, width):
    for axis, dim in sides:
        count = lax.axis_size(axis)
        ends = count - 1
        head = lax.slice_in_dim(cells, 0, width, axis=dim)
        tail = lax.slice_in_dim(cells, cells.shape[dim] - width, cells.shape[dim], axis=dim)
        cells = jnp.concatenate(
            [
                lax.ppermute(tail, axis, [(i, (i + 1) % count) for i in range(ends)]),
                cells,
                lax.ppermute(head, axis, [((i + 1) % count, i) for i in range(ends)]),
            ],
            axis=dim,
        )
    return cells


def stencil_inner(padded):
    centre = padded[:, 1:-1, 1:-1]
    beside = padded[:, 2:, 1:-1] + padded[:, :-2, 1:-1]
    beside = beside + padded[:, 1:-1, 2:] + padded[:, 1:-1, :-2]
    zeros_face = jnp.zeros(centre.shape[:3] + (1,), centre.dtype)
    upper_z = jnp.concatenate([centre[..., 1:], zeros_face], axis=3)
    lower_z = jnp.concatenate([zeros_face, centre[..., :-1]], axis=3)
    return 6.0 * centre - (beside + upper_z + lower_z)


def apply_operator(values):
    padded = with_halo(values, (("grp", 1), ("mem", 2)), 1)
    return stencil_inner(padded)


def restrict_blocks(residual, aggregate):
    blk_x, blk_y, blk_z = aggregate.shape
    sides = residual.shape[0]
    means = (
        residual.reshape(sides, blk_x, 4, blk_y, 4, blk_z, 4)
        .mean(axis=(2, 4, 6))
        .reshape(sides, -1)
    )
    summed = jax.ops.segment_sum(means.T, aggregate.reshape(-1), num_segments=NC)
    return summed.T


def prolong_blocks(coarse_fix, ids, valid):
    blk_x, blk_y, blk_z = ids.shape
    sides = coarse_fix.shape[0]
    picked = jnp.take(coarse_fix, ids.reshape(-1), axis=1) * valid.reshape(1, -1)
    picked = picked.reshape(sides, blk_x, 1, blk_y, 1, blk_z, 1)
    spread = jnp.broadcast_to(picked, (sides, blk_x, 4, blk_y, 4, blk_z, 4))
    return spread.reshape(sides, blk_x * 4, blk_y * 4, blk_z * 4)


def solve_blocks(coarse_rhs, factors):
    block_count = factors.shape[0]
    block_size = factors.shape[1]
    sides = coarse_rhs.shape[0]
    blocks = coarse_rhs.reshape(sides, block_count, block_size)
    inner = jnp.einsum("kbj,bij->kbi", blocks, factors, precision=lax.Precision.HIGHEST)
    result = jnp.einsum("kbi,bij->kbj", inner, factors, precision=lax.Precision.HIGHEST)
    return result.reshape(sides, block_count * block_size)


def shards(forcing, aggregate, factors):
    weight = relaxation / 6.0
    smoothed = weight * forcing
    for repeat in range(PRE - 1):
        smoothed = smoothed + weight * (forcing - apply_operator(smoothed))
    residual = forcing - apply_operator(smoothed)
    partial_value = restrict_blocks(residual, aggregate)
    coarse_rhs = lax.psum(partial_value, ("grp", "mem"))
    all_factors = lax.all_gather(factors, "mem", axis=0, tiled=True)
    coarse_fix = solve_blocks(coarse_rhs, all_factors)
    lifted = prolong_blocks(coarse_fix, aggregate, jnp.ones(aggregate.shape, jnp.float32))
    correction = lifted - weight * apply_operator(lifted)
    solution = smoothed + correction
    for repeat in range(POST):
        solution = solution + weight * (forcing - apply_operator(solution))
    return solution


def solution(mesh):
    placed = (P(None, "grp", "mem", None), P("grp", "mem", None), P("mem", None, None))
    return jax.shard_map(
        shards, mesh=mesh, in_specs=placed, out_specs=P(None, "grp", "mem", None), check_vma=False
    )
```

profile of v0, /device:TPU:8, one launch (start us, length us, event | category | flops | bytes accessed | tf_op | source)
XLA Modules:
  0.0 380.2 jit_solution(7049673006676737177)
XLA Ops:
  7.4 1.8 broadcast_multiply_fusion
  9.2 2.7 collective-permute-start
  11.9 1.9 collective-permute-start.1
  14.4 4.7 %collective-permute-done.1 = f32[16,1,16,128]{3,2,1,0:T(8,128)S(1)} collective-permute-done((f32[16,1,16,128]{3,2,1,0:T(8,128)S(1)}, f32[16,1,16,128]{3,2,1,0:T(8,128)S(1)}, u32[]{:S(2)}, u32[]{:S(2)}) %collective-permute-start.1) | collective-permute-done | bytes 131104 | tf_op jit(solution)/shard_map/ppermute | solution.py:20
  19.3 3.4 collective-permute-start.3
  22.8 1.4 collective-permute-start.2
  24.2 0.8 fusion.64
  25.6 4.4 %collective-permute-done.2 = f32[16,18,1,128]{3,0,2,1:T(8,128)S(1)} collective-permute-done((f32[16,18,1,128]{3,0,2,1:T(8,128)S(1)}, f32[16,18,1,128]{3,0,2,1:T(8,128)S(1)}, u32[]{:S(2)}, u32[]{:S(2)}) %collective-permute-start.2) | collective-permute-done | bytes 147488 | tf_op jit(solution)/shard_map/ppermute | solution.py:22
  30.1 2.1 fusion.49
  32.2 1.9 collective-permute-start.4
  34.2 2.4 collective-permute-start.5
  36.7 4.7 %collective-permute-done.5 = f32[16,1,16,128]{3,2,1,0:T(8,128)S(1)} collective-permute-done((f32[16,1,16,128]{3,2,1,0:T(8,128)S(1)}, f32[16,1,16,128]{3,2,1,0:T(8,128)S(1)}, u32[]{:S(2)}, u32[]{:S(2)}) %collective-permute-start.5) | collective-permute-done | bytes 131104 | tf_op jit(solution)/shard_map/ppermute | solution.py:20
  41.6 1.5 collective-permute-start.7
  43.1 1.3 collective-permute-start.6
  44.4 0.8 fusion.62
  45.9 4.3 %collective-permute-done.6 = f32[16,18,1,128]{3,0,2,1:T(8,128)S(1)} collective-permute-done((f32[16,18,1,128]{3,0,2,1:T(8,128)S(1)}, f32[16,18,1,128]{3,0,2,1:T(8,128)S(1)}, u32[]{:S(2)}, u32[]{:S(2)}) %collective-permute-start.6) | collective-permute-done | bytes 147488 | tf_op jit(solution)/shard_map/ppermute | solution.py:22
  50.3 2.0 fusion.40
  52.3 1.9 collective-permute-start.8
  54.3 2.4 collective-permute-start.9
  56.8 4.7 %collective-permute-done.9 = f32[16,1,16,128]{3,2,1,0:T(8,128)S(1)} collective-permute-done((f32[16,1,16,128]{3,2,1,0:T(8,128)S(1)}, f32[16,1,16,128]{3,2,1,0:T(8,128)S(1)}, u32[]{:S(2)}, u32[]{:S(2)}) %collective-permute-start.9) | collective-permute-done | bytes 131104 | tf_op jit(solution)/shard_map/ppermute | solution.py:20
  61.7 1.5 collective-permute-start.11
  63.2 1.4 collective-permute-start.10
  64.6 0.7 fusion.60
  66.0 4.4 %collective-permute-done.10 = f32[16,18,1,128]{3,0,2,1:T(8,128)S(1)} collective-permute-done((f32[16,18,1,128]{3,0,2,1:T(8,128)S(1)}, f32[16,18,1,128]{3,0,2,1:T(8,128)S(1)}, u32[]{:S(2)}, u32[]{:S(2)}) %collective-permute-start.10) | collective-permute-done | bytes 147488 | tf_op jit(solution)/shard_map/ppermute | solution.py:22
  70.5 2.8 fusion.31
  73.4 10.0 %copy.356 = f32[16,16,16,128]{0,3,2,1:T(8,128)} copy(f32[16,16,16,128]{3,2,1,0:T(8,128)} %fusion.31) | data formatting | bytes 4194304 | tf_op jit(solution)/shard_map/sub | solution.py:80
  83.4 9.4 %reduce_sum.9 = f32[16,4,4,32]{0,3,2,1:T(8,128)S(1)} reduce(f32[16,4,4,4,4,32,4]{0,6,5,4,3,2,1:T(4,128)} %bitcast.23, f32[]{:T(128)} %constant.11.clone.1), dimensions={2,4,6}, to_apply=%region_0.0 | reduce | flops 516096 | bytes 2129924 | tf_op jit(solution)/shard_map/reduce_sum | solution.py:49
  92.8 4.4 %scatter_custom_fusion = f32[8192,16]{1,0:T(8,128)} fusion(s32[512]{0:T(512)S(1)} %reshape.77, f32[512,16]{1,0:T(8,128)S(1)} %bitcast.27, f32[]{:T(128)} %constant.11.clone.1), kind=kCustom, calls=%fused_computation.102 | custom fusion | flops 8192 | bytes 524292 | tf_op jit(solution)/shard_map/scatter-add | solution.py:52
  97.2 3.5 copy.358
  101.4 166.7 %all-reduce.14.cloned.1.call-done = f32[16,64,128]{2,0,1:T(8,128)} async-done(((f32[16,64,128]{2,0,1:T(8,128)}), f32[16,64,128]{2,0,1:T(8,128)}) %all-reduce.14.cloned.1.call-update) | async-done | bytes 524304 | tf_op jit(solution)/shard_map/psum | solution.py:82
  268.1 8.6 %convolution_bitcast_fusion.1 = f32[16,64,128]{2,0,1:T(8,128)S(1)} fusion(f32[16,64,128]{2,0,1:T(8,128)} %all-reduce.14.cloned.1.call-done, f32[64,128,128]{2,1,0:T(8,128)} %all-gather.2.cloned.1.call-done), kind=kOutput, calls=%fused_computation.105 | convolution fusion | flops 201326592 | bytes 5242880 | tf_op jit(solution)/shard_map/kbj,bij->kbi/dot_general | solution.py:70
  276.8 3.8 convolution_bitcast_fusion
  280.6 2.6 copy.384
  283.2 3.2 gather_fusion
  286.5 3.9 %broadcast_in_dim.21 = f32[16,4,4,4,4,32,4]{0,6,5,4,3,2,1:T(4,128)S(1)} broadcast(f32[16,4,4,32]{0,3,2,1:T(8,128)S(1)} %broadcast_select_fusion), dimensions={0,1,3,5} | broadcast | bytes 2129920 | tf_op jit(solution)/shard_map/broadcast_in_dim | solution.py:61
  290.4 5.7 %copy-done = f32[16,4,4,4,4,32,4]{0,6,5,4,3,2,1:T(4,128)} copy-done((f32[16,4,4,4,4,32,4]{0,6,5,4,3,2,1:T(4,128)}, f32[16,4,4,4,4,32,4]{0,6,5,4,3,2,1:T(4,128)S(1)}, u32[]{:S(2)}) %copy-start) | copy-done | bytes 2097176
  296.2 1.2 fusion.54
  297.3 1.5 copy.362
  298.9 2.0 collective-permute-start.12
  301.2 2.3 collective-permute-start.13
  303.5 11.0 %copy.373 = f32[16,16,16,128]{3,2,1,0:T(8,128)} copy(f32[16,16,16,128]{0,3,2,1:T(8,128)} %bitcast.22) | data formatting | bytes 4194304 | tf_op jit(solution)/shard_map/reshape | solution.py:62
  314.5 1.9 pad_maximum_fusion.56
  316.5 3.4 collective-permute-start.15
  319.9 1.3 collective-permute-start.14
  321.2 0.8 fusion.59
  322.0 1.3 collective-permute-done.15
  323.5 4.0 %collective-permute-done.14 = f32[16,18,1,128]{3,0,2,1:T(8,128)S(1)} collective-permute-done((f32[16,18,1,128]{3,0,2,1:T(8,128)S(1)}, f32[16,18,1,128]{3,0,2,1:T(8,128)S(1)}, u32[]{:S(2)}, u32[]{:S(2)}) %collective-permute-start.14) | collective-permute-done | bytes 147488 | tf_op jit(solution)/shard_map/ppermute | solution.py:22
  327.6 2.0 fusion.24
  329.6 3.8 %collective-permute-start.16 = (f32[16,1,16,128]{3,2,1,0:T(8,128)S(1)}, f32[16,1,16,128]{3,2,1,0:T(8,128)S(1)}, u32[]{:S(2)}, u32[]{:S(2)}) collective-permute-start(f32[16,1,16,128]{3,2,1,0:T(8,128)S(1)} %get-tuple-element.26), channel_id=1, source_target_pairs={{2,0},{4,2},{6,4},{8,6},{10,8},{12,10},{14,12},{16,14},{18,16},{20... | collective-permute-start | bytes 393224 | tf_op jit(solution)/shard_map/ppermute | solution.py:22
  333.5 1.9 collective-permute-start.17
  336.0 4.7 %collective-permute-done.17 = f32[16,1,16,128]{3,2,1,0:T(8,128)S(1)} collective-permute-done((f32[16,1,16,128]{3,2,1,0:T(8,128)S(1)}, f32[16,1,16,128]{3,2,1,0:T(8,128)S(1)}, u32[]{:S(2)}, u32[]{:S(2)}) %collective-permute-start.17) | collective-permute-done | bytes 131104 | tf_op jit(solution)/shard_map/ppermute | solution.py:20
  340.9 1.5 collective-permute-start.19
  342.4 1.6 collective-permute-start.18
  344.0 0.8 fusion.57
  345.1 4.4 %collective-permute-done.18 = f32[16,18,1,128]{3,0,2,1:T(8,128)S(1)} collective-permute-done((f32[16,18,1,128]{3,0,2,1:T(8,128)S(1)}, f32[16,18,1,128]{3,0,2,1:T(8,128)S(1)}, u32[]{:S(2)}, u32[]{:S(2)}) %collective-permute-start.18) | collective-permute-done | bytes 147488 | tf_op jit(solution)/shard_map/ppermute | solution.py:22
  349.7 2.0 fusion.15
  351.8 1.9 collective-permute-start.20
  353.7 2.4 collective-permute-start.21
  356.2 4.7 %collective-permute-done.21 = f32[16,1,16,128]{3,2,1,0:T(8,128)S(1)} collective-permute-done((f32[16,1,16,128]{3,2,1,0:T(8,128)S(1)}, f32[16,1,16,128]{3,2,1,0:T(8,128)S(1)}, u32[]{:S(2)}, u32[]{:S(2)}) %collective-permute-start.21) | collective-permute-done | bytes 131104 | tf_op jit(solution)/shard_map/ppermute | solution.py:20
  361.1 1.5 collective-permute-start.23
  362.6 1.3 collective-permute-start.22
  363.9 0.8 fusion.55
  365.4 4.3 %collective-permute-done.22 = f32[16,18,1,128]{3,0,2,1:T(8,128)S(1)} collective-permute-done((f32[16,18,1,128]{3,0,2,1:T(8,128)S(1)}, f32[16,18,1,128]{3,0,2,1:T(8,128)S(1)}, u32[]{:S(2)}, u32[]{:S(2)}) %collective-permute-start.22) | collective-permute-done | bytes 147488 | tf_op jit(solution)/shard_map/ppermute | solution.py:22
  369.8 3.0 fusion.6
  (72 shorter events, 7.9 us)
Async XLA Ops:
  7.4 260.8 %all-reduce.14.cloned.1.call-start = ((), (), s32[]{:S(2)}) async-start(), calls=%async_computation | async-start | bytes 1048576 | tf_op jit(solution)/shard_map/psum | solution.py:82
  9.2 5.2 %collective-permute-start = (f32[16,1,16,128]{3,2,1,0:T(8,128)S(1)}, f32[16,1,16,128]{3,2,1,0:T(8,128)S(1)}, u32[]{:S(2)}, u32[]{:S(2)}) collective-permute-start(f32[16,1,16,128]{3,2,1,0:T(8,128)S(1)} %get-tuple-element.40), channel_id=1, source_target_pairs={{2,0},{4,2},{6,4},{8,6},{10,8},{12,10},{14,12},{16,14},{18,16},{20... | collective-permute-start | bytes 393224 | tf_op jit(solution)/shard_map/ppermute | solution.py:22
  11.9 7.2 %collective-permute-start.1 = (f32[16,1,16,128]{3,2,1,0:T(8,128)S(1)}, f32[16,1,16,128]{3,2,1,0:T(8,128)S(1)}, u32[]{:S(2)}, u32[]{:S(2)}) collective-permute-start(f32[16,1,16,128]{3,2,1,0:T(8,128)S(1)} %get-tuple-element.39), channel_id=1, source_target_pairs={{0,2},{2,4},{4,6},{6,8},{8,10},{10,12},{12,14},{14,16},{16,18},{18... | collective-permute-start | bytes 393224 | tf_op jit(solution)/shard_map/ppermute | solution.py:20
  19.3 6.1 %collective-permute-start.3 = (f32[16,18,1,128]{3,0,2,1:T(8,128)S(1)}, f32[16,18,1,128]{3,0,2,1:T(8,128)S(1)}, u32[]{:S(2)}, u32[]{:S(2)}) collective-permute-start(f32[16,18,1,128]{3,0,2,1:T(8,128)S(1)} %copy.346), channel_id=1, source_target_pairs={{0,1},{2,3},{4,5},{6,7},{8,9},{10,11},{12,13},{14,15},{16,17},{18,... | collective-permute-start | bytes 442376 | tf_op jit(solution)/shard_map/ppermute | solution.py:20
  22.8 7.3 %copy-start.1 = (f32[16,16,16,128]{3,2,1,0:T(8,128)S(1)}, f32[16,16,16,128]{3,2,1,0:T(8,128)}, u32[]{:S(2)}) copy-start(f32[16,16,16,128]{3,2,1,0:T(8,128)} %param.3) | copy-start | bytes 6291460
  22.8 7.2 %collective-permute-start.2 = (f32[16,18,1,128]{3,0,2,1:T(8,128)S(1)}, f32[16,18,1,128]{3,0,2,1:T(8,128)S(1)}, u32[]{:S(2)}, u32[]{:S(2)}) collective-permute-start(f32[16,18,1,128]{3,0,2,1:T(8,128)S(1)} %copy.344), channel_id=1, source_target_pairs={{1,0},{3,2},{5,4},{7,6},{9,8},{11,10},{13,12},{15,14},{17,16},{19,... | collective-permute-start | bytes 442376 | tf_op jit(solution)/shard_map/ppermute | solution.py:22
  32.2 4.4 %collective-permute-start.4 = (f32[16,1,16,128]{3,2,1,0:T(8,128)S(1)}, f32[16,1,16,128]{3,2,1,0:T(8,128)S(1)}, u32[]{:S(2)}, u32[]{:S(2)}) collective-permute-start(f32[16,1,16,128]{3,2,1,0:T(8,128)S(1)} %get-tuple-element.36), channel_id=1, source_target_pairs={{2,0},{4,2},{6,4},{8,6},{10,8},{12,10},{14,12},{16,14},{18,16},{20... | collective-permute-start | bytes 393224 | tf_op jit(solution)/shard_map/ppermute | solution.py:22
  34.2 7.2 %collective-permute-start.5 = (f32[16,1,16,128]{3,2,1,0:T(8,128)S(1)}, f32[16,1,16,128]{3,2,1,0:T(8,128)S(1)}, u32[]{:S(2)}, u32[]{:S(2)}) collective-permute-start(f32[16,1,16,128]{3,2,1,0:T(8,128)S(1)} %get-tuple-element.35), channel_id=1, source_target_pairs={{0,2},{2,4},{4,6},{6,8},{8,10},{10,12},{12,14},{14,16},{16,18},{18... | collective-permute-start | bytes 393224 | tf_op jit(solution)/shard_map/ppermute | solution.py:20
  41.6 4.1 %collective-permute-start.7 = (f32[16,18,1,128]{3,0,2,1:T(8,128)S(1)}, f32[16,18,1,128]{3,0,2,1:T(8,128)S(1)}, u32[]{:S(2)}, u32[]{:S(2)}) collective-permute-start(f32[16,18,1,128]{3,0,2,1:T(8,128)S(1)} %copy.350), channel_id=1, source_target_pairs={{0,1},{2,3},{4,5},{6,7},{8,9},{10,11},{12,13},{14,15},{16,17},{18,... | collective-permute-start | bytes 442376 | tf_op jit(solution)/shard_map/ppermute | solution.py:20
  43.1 7.0 %collective-permute-start.6 = (f32[16,18,1,128]{3,0,2,1:T(8,128)S(1)}, f32[16,18,1,128]{3,0,2,1:T(8,128)S(1)}, u32[]{:S(2)}, u32[]{:S(2)}) collective-permute-start(f32[16,18,1,128]{3,0,2,1:T(8,128)S(1)} %copy.348), channel_id=1, source_target_pairs={{1,0},{3,2},{5,4},{7,6},{9,8},{11,10},{13,12},{15,14},{17,16},{19,... | collective-permute-start | bytes 442376 | tf_op jit(solution)/shard_map/ppermute | solution.py:22
  50.3 6.4 %copy-start.6 = (s32[4,4,32]{2,1,0:T(4,128)S(1)}, s32[4,4,32]{2,1,0:T(4,128)}, u32[]{:S(2)}) copy-start(s32[4,4,32]{2,1,0:T(4,128)} %param.4) | copy-start | bytes 6148
  52.3 4.4 %collective-permute-start.8 = (f32[16,1,16,128]{3,2,1,0:T(8,128)S(1)}, f32[16,1,16,128]{3,2,1,0:T(8,128)S(1)}, u32[]{:S(2)}, u32[]{:S(2)}) collective-permute-start(f32[16,1,16,128]{3,2,1,0:T(8,128)S(1)} %get-tuple-element.32), channel_id=1, source_target_pairs={{2,0},{4,2},{6,4},{8,6},{10,8},{12,10},{14,12},{16,14},{18,16},{20... | collective-permute-start | bytes 393224 | tf_op jit(solution)/shard_map/ppermute | solution.py:22
  54.3 7.2 %collective-permute-start.9 = (f32[16,1,16,128]{3,2,1,0:T(8,128)S(1)}, f32[16,1,16,128]{3,2,1,0:T(8,128)S(1)}, u32[]{:S(2)}, u32[]{:S(2)}) collective-permute-start(f32[16,1,16,128]{3,2,1,0:T(8,128)S(1)} %get-tuple-element.31), channel_id=1, source_target_pairs={{0,2},{2,4},{4,6},{6,8},{8,10},{10,12},{12,14},{14,16},{16,18},{18... | collective-permute-start | bytes 393224 | tf_op jit(solution)/shard_map/ppermute | solution.py:20
  61.7 4.1 %collective-permute-start.11 = (f32[16,18,1,128]{3,0,2,1:T(8,128)S(1)}, f32[16,18,1,128]{3,0,2,1:T(8,128)S(1)}, u32[]{:S(2)}, u32[]{:S(2)}) collective-permute-start(f32[16,18,1,128]{3,0,2,1:T(8,128)S(1)} %copy.354), channel_id=1, source_target_pairs={{0,1},{2,3},{4,5},{6,7},{8,9},{10,11},{12,13},{14,15},{16,17},{18,... | collective-permute-start | bytes 442376 | tf_op jit(solution)/shard_map/ppermute | solution.py:20
  63.2 7.3 %copy-start.2 = (f32[16,16,16,128]{3,2,1,0:T(8,128)S(1)}, f32[16,16,16,128]{3,2,1,0:T(8,128)}, u32[]{:S(2)}) copy-start(f32[16,16,16,128]{3,2,1,0:T(8,128)} %param.3) | copy-start | bytes 6291460
  63.2 7.2 %collective-permute-start.10 = (f32[16,18,1,128]{3,0,2,1:T(8,128)S(1)}, f32[16,18,1,128]{3,0,2,1:T(8,128)S(1)}, u32[]{:S(2)}, u32[]{:S(2)}) collective-permute-start(f32[16,18,1,128]{3,0,2,1:T(8,128)S(1)} %copy.352), channel_id=1, source_target_pairs={{1,0},{3,2},{5,4},{7,6},{9,8},{11,10},{13,12},{15,14},{17,16},{19,... | collective-permute-start | bytes 442376 | tf_op jit(solution)/shard_map/ppermute | solution.py:22
  100.7 167.4 %all-gather.2.cloned.1.call-start = ((), (), s32[]{:S(2)}) async-start(), calls=%async_computation.1 | async-start | bytes 6291456 | tf_op jit(solution)/shard_map/all_gather | solution.py:83
  268.1 8.6 %copy-start.5 = (f32[64,128,128]{2,1,0:T(8,128)S(1)}, f32[64,128,128]{2,1,0:T(8,128)}, u32[]{:S(2)}) copy-start(f32[64,128,128]{2,1,0:T(8,128)} %all-gather.2.cloned.1.call-done) | copy-start | bytes 12582916
  290.4 5.8 %copy-start = (f32[16,4,4,4,4,32,4]{0,6,5,4,3,2,1:T(4,128)}, f32[16,4,4,4,4,32,4]{0,6,5,4,3,2,1:T(4,128)S(1)}, u32[]{:S(2)}) copy-start(f32[16,4,4,4,4,32,4]{0,6,5,4,3,2,1:T(4,128)S(1)} %broadcast_in_dim.21) | copy-start | bytes 6291460
  298.9 15.7 %collective-permute-start.12 = (f32[16,1,16,128]{3,2,1,0:T(8,128)S(1)}, f32[16,1,16,128]{3,2,1,0:T(8,128)S(1)}, u32[]{:S(2)}, u32[]{:S(2)}) collective-permute-start(f32[16,1,16,128]{3,2,1,0:T(8,128)S(1)} %copy.362), channel_id=1, source_target_pairs={{2,0},{4,2},{6,4},{8,6},{10,8},{12,10},{14,12},{16,14},{18,16},{20... | collective-permute-start | bytes 393224 | tf_op jit(solution)/shard_map/ppermute | solution.py:22
  301.2 13.3 %collective-permute-start.13 = (f32[16,1,16,128]{3,2,1,0:T(8,128)S(1)}, f32[16,1,16,128]{3,2,1,0:T(8,128)S(1)}, u32[]{:S(2)}, u32[]{:S(2)}) collective-permute-start(f32[16,1,16,128]{3,2,1,0:T(8,128)S(1)} %copy.364), channel_id=1, source_target_pairs={{0,2},{2,4},{4,6},{6,8},{8,10},{10,12},{12,14},{14,16},{16,18},{18... | collective-permute-start | bytes 393224 | tf_op jit(solution)/shard_map/ppermute | solution.py:20
  314.5 6.7 %copy-start.4 = (f32[16,16,16,128]{3,2,1,0:T(8,128)S(1)}, f32[16,16,16,128]{3,2,1,0:T(8,128)}, u32[]{:S(2)}) copy-start(f32[16,16,16,128]{3,2,1,0:T(8,128)} %copy.373) | copy-start | bytes 6291460
  316.5 6.8 %collective-permute-start.15 = (f32[16,18,1,128]{3,0,2,1:T(8,128)S(1)}, f32[16,18,1,128]{3,0,2,1:T(8,128)S(1)}, u32[]{:S(2)}, u32[]{:S(2)}) collective-permute-start(f32[16,18,1,128]{3,0,2,1:T(8,128)S(1)} %copy.369), channel_id=1, source_target_pairs={{0,1},{2,3},{4,5},{6,7},{8,9},{10,11},{12,13},{14,15},{16,17},{18,... | collective-permute-start | bytes 442376 | tf_op jit(solution)/shard_map/ppermute | solution.py:20
  319.9 7.5 %collective-permute-start.14 = (f32[16,18,1,128]{3,0,2,1:T(8,128)S(1)}, f32[16,18,1,128]{3,0,2,1:T(8,128)S(1)}, u32[]{:S(2)}, u32[]{:S(2)}) collective-permute-start(f32[16,18,1,128]{3,0,2,1:T(8,128)S(1)} %copy.367), channel_id=1, source_target_pairs={{1,0},{3,2},{5,4},{7,6},{9,8},{11,10},{13,12},{15,14},{17,16},{19,... | collective-permute-start | bytes 442376 | tf_op jit(solution)/shard_map/ppermute | solution.py:22
  329.6 6.3 %collective-permute-start.16 = (f32[16,1,16,128]{3,2,1,0:T(8,128)S(1)}, f32[16,1,16,128]{3,2,1,0:T(8,128)S(1)}, u32[]{:S(2)}, u32[]{:S(2)}) collective-permute-start(f32[16,1,16,128]{3,2,1,0:T(8,128)S(1)} %get-tuple-element.26), channel_id=1, source_target_pairs={{2,0},{4,2},{6,4},{8,6},{10,8},{12,10},{14,12},{16,14},{18,16},{20... | collective-permute-start | bytes 393224 | tf_op jit(solution)/shard_map/ppermute | solution.py:22
  333.5 7.2 %collective-permute-start.17 = (f32[16,1,16,128]{3,2,1,0:T(8,128)S(1)}, f32[16,1,16,128]{3,2,1,0:T(8,128)S(1)}, u32[]{:S(2)}, u32[]{:S(2)}) collective-permute-start(f32[16,1,16,128]{3,2,1,0:T(8,128)S(1)} %get-tuple-element.25), channel_id=1, source_target_pairs={{0,2},{2,4},{4,6},{6,8},{8,10},{10,12},{12,14},{14,16},{16,18},{18... | collective-permute-start | bytes 393224 | tf_op jit(solution)/shard_map/ppermute | solution.py:20
  340.9 4.1 %collective-permute-start.19 = (f32[16,18,1,128]{3,0,2,1:T(8,128)S(1)}, f32[16,18,1,128]{3,0,2,1:T(8,128)S(1)}, u32[]{:S(2)}, u32[]{:S(2)}) collective-permute-start(f32[16,18,1,128]{3,0,2,1:T(8,128)S(1)} %copy.376), channel_id=1, source_target_pairs={{0,1},{2,3},{4,5},{6,7},{8,9},{10,11},{12,13},{14,15},{16,17},{18,... | collective-permute-start | bytes 442376 | tf_op jit(solution)/shard_map/ppermute | solution.py:20
  342.4 7.3 %copy-start.3 = (f32[16,16,16,128]{3,2,1,0:T(8,128)S(1)}, f32[16,16,16,128]{3,2,1,0:T(8,128)}, u32[]{:S(2)}) copy-start(f32[16,16,16,128]{3,2,1,0:T(8,128)} %param.3) | copy-start | bytes 6291460
  342.4 7.2 %collective-permute-start.18 = (f32[16,18,1,128]{3,0,2,1:T(8,128)S(1)}, f32[16,18,1,128]{3,0,2,1:T(8,128)S(1)}, u32[]{:S(2)}, u32[]{:S(2)}) collective-permute-start(f32[16,18,1,128]{3,0,2,1:T(8,128)S(1)} %copy.374), channel_id=1, source_target_pairs={{1,0},{3,2},{5,4},{7,6},{9,8},{11,10},{13,12},{15,14},{17,16},{19,... | collective-permute-start | bytes 442376 | tf_op jit(solution)/shard_map/ppermute | solution.py:22
  351.8 4.4 %collective-permute-start.20 = (f32[16,1,16,128]{3,2,1,0:T(8,128)S(1)}, f32[16,1,16,128]{3,2,1,0:T(8,128)S(1)}, u32[]{:S(2)}, u32[]{:S(2)}) collective-permute-start(f32[16,1,16,128]{3,2,1,0:T(8,128)S(1)} %get-tuple-element.22), channel_id=1, source_target_pairs={{2,0},{4,2},{6,4},{8,6},{10,8},{12,10},{14,12},{16,14},{18,16},{20... | collective-permute-start | bytes 393224 | tf_op jit(solution)/shard_map/ppermute | solution.py:22
  353.7 7.2 %collective-permute-start.21 = (f32[16,1,16,128]{3,2,1,0:T(8,128)S(1)}, f32[16,1,16,128]{3,2,1,0:T(8,128)S(1)}, u32[]{:S(2)}, u32[]{:S(2)}) collective-permute-start(f32[16,1,16,128]{3,2,1,0:T(8,128)S(1)} %get-tuple-element.21), channel_id=1, source_target_pairs={{0,2},{2,4},{4,6},{6,8},{8,10},{10,12},{12,14},{14,16},{16,18},{18... | collective-permute-start | bytes 393224 | tf_op jit(solution)/shard_map/ppermute | solution.py:20
  361.1 4.1 %collective-permute-start.23 = (f32[16,18,1,128]{3,0,2,1:T(8,128)S(1)}, f32[16,18,1,128]{3,0,2,1:T(8,128)S(1)}, u32[]{:S(2)}, u32[]{:S(2)}) collective-permute-start(f32[16,18,1,128]{3,0,2,1:T(8,128)S(1)} %copy.380), channel_id=1, source_target_pairs={{0,1},{2,3},{4,5},{6,7},{8,9},{10,11},{12,13},{14,15},{16,17},{18,... | collective-permute-start | bytes 442376 | tf_op jit(solution)/shard_map/ppermute | solution.py:20
  362.6 7.0 %collective-permute-start.22 = (f32[16,18,1,128]{3,0,2,1:T(8,128)S(1)}, f32[16,18,1,128]{3,0,2,1:T(8,128)S(1)}, u32[]{:S(2)}, u32[]{:S(2)}) collective-permute-start(f32[16,18,1,128]{3,0,2,1:T(8,128)S(1)} %copy.378), channel_id=1, source_target_pairs={{1,0},{3,2},{5,4},{7,6},{9,8},{11,10},{13,12},{15,14},{17,16},{19,... | collective-permute-start | bytes 442376 | tf_op jit(solution)/shard_map/ppermute | solution.py:22
Sparse Core Ops, SparseCore 0:
  100.8 167.2 all-reduce.13
Sparse Core Ops, SparseCore 1:
  102.7 56.0 all-gather.1
where the time goes:
time: 381 us; the launch traced here: 380 us
  waiting for transfers between devices  221 us (58%)
  local copies, waits for them, and re-layouts  49.7 us (13%)
  starting transfers between devices  48.9 us (13%)
  other arithmetic  32.7 us (9%)
  between operations  15.5 us (4%)
  matrix products  12.4 us (3%)
    psum x1, waiting for transfers between devices, shards(): coarse_rhs = lax.psum(partial_value, ('grp', 'mem'))  167 us
    ppermute x12, waiting for transfers between devices, with_halo(): lax.ppermute(tail, axis, [(i, (i + 1) % count) for i in range(ends)])  27 us
    ppermute x12, waiting for transfers between devices, with_halo(): lax.ppermute(head, axis, [((i + 1) % count, i) for i in range(ends)])  27 us
    ppermute x12, starting transfers between devices, with_halo(): lax.ppermute(tail, axis, [(i, (i + 1) % count) for i in range(ends)])  26.1 us
    ppermute x12, starting transfers between devices, with_halo(): lax.ppermute(head, axis, [((i + 1) % count, i) for i in range(ends)])  22.7 us
    reshape x1, local copies, waits for them, and re-layouts, prolong_blocks(): return spread.reshape(sides, blk_x * 4, blk_y * 4, blk_z * 4)  11 us
    sub x1, local copies, waits for them, and re-layouts, shards(): residual = forcing - apply_operator(smoothed)  10 us
    reduce_sum x1, other arithmetic, restrict_blocks(): means = residual.reshape(sides, blk_x, 4, blk_y, 4, blk_z, 4).mean(axis=(...  9.37 us
  transfers between devices with their start and end apart: 26, of which 22 were waited for; matrix products, arithmetic and copies ran while one was open for 4% of the time, Pallas kernels for 0%

commit v1 on v0

--- a/solution.py
+++ b/solution.py
@@ -79,7 +79,7 @@
         smoothed = smoothed + weight * (forcing - apply_operator(smoothed))
     residual = forcing - apply_operator(smoothed)
     partial_value = restrict_blocks(residual, aggregate)
-    coarse_rhs = lax.psum(partial_value, ("grp", "mem"))
+    coarse_rhs = jax.lax.psum(jax.lax.psum(partial_value, "mem"), "grp")
     all_factors = lax.all_gather(factors, "mem", axis=0, tiled=True)
     coarse_fix = solve_blocks(coarse_rhs, all_factors)
     lifted = prolong_blocks(coarse_fix, aggregate, jnp.ones(aggregate.shape, jnp.float32))

time: 381 us -> 468 us (1.23)
  waiting for transfers between devices: 221 us -> 311 us
    all_gather x1, waiting for transfers between devices: 0.01 us -> 57.4 us  [shards(): all_factors = lax.all_gather(factors, 'mem', axis=0, tiled=True)]
    psum x1 -> x2, waiting for transfers between devices: 167 us -> 199 us  [shards(): coarse_rhs = jax.lax.psum(jax.lax.psum(partial_value, 'mem'), 'grp')]
  transfers between devices with their start and end apart: 26 -> 27, of which waited for: 22 -> 24; matrix products, arithmetic and copies ran while one was open for 4% -> 4% of each run, Pallas kernels for 0% -> 0%
where the time goes in v1:
time: 468 us; the launch traced here: 467 us
  waiting for transfers between devices  311 us (66%)
  local copies, waits for them, and re-layouts  49.7 us (11%)
  starting transfers between devices  47.7 us (10%)
  other arithmetic  32.6 us (7%)
  between operations  13.7 us (3%)
  matrix products  12.4 us (3%)
    psum x2, waiting for transfers between devices, shards(): coarse_rhs = jax.lax.psum(jax.lax.psum(partial_value, 'mem'), 'grp')  199 us
    all_gather x1, waiting for transfers between devices, shards(): all_factors = lax.all_gather(factors, 'mem', axis=0, tiled=True)  57.4 us
    ppermute x12, waiting for transfers between devices, with_halo(): lax.ppermute(tail, axis, [(i, (i + 1) % count) for i in range(ends)])  27.7 us
    ppermute x12, waiting for transfers between devices, with_halo(): lax.ppermute(head, axis, [((i + 1) % count, i) for i in range(ends)])  27 us
    ppermute x12, starting transfers between devices, with_halo(): lax.ppermute(tail, axis, [(i, (i + 1) % count) for i in range(ends)])  25 us
    ppermute x12, starting transfers between devices, with_halo(): lax.ppermute(head, axis, [((i + 1) % count, i) for i in range(ends)])  22.4 us
    reshape x1, local copies, waits for them, and re-layouts, prolong_blocks(): return spread.reshape(sides, blk_x * 4, blk_y * 4, blk_z * 4)  11 us
    sub x1, local copies, waits for them, and re-layouts, shards(): residual = forcing - apply_operator(smoothed)  10 us
  transfers between devices with their start and end apart: 27, of which 24 were waited for; matrix products, arithmetic and copies ran while one was open for 4% of the time, Pallas kernels for 0%

profile of v1, /device:TPU:8, one launch (start us, length us, event | category | flops | bytes accessed | tf_op | source)
XLA Modules:
  0.0 467.4 jit_solution(8844465992967161503)
XLA Ops:
  6.5 1.8 broadcast_multiply_fusion
  8.4 2.7 collective-permute-start
  11.1 1.9 collective-permute-start.1
  13.6 4.7 %collective-permute-done.1 = f32[16,1,16,128]{3,2,1,0:T(8,128)S(1)} collective-permute-done((f32[16,1,16,128]{3,2,1,0:T(8,128)S(1)}, f32[16,1,16,128]{3,2,1,0:T(8,128)S(1)}, u32[]{:S(2)}, u32[]{:S(2)}) %collective-permute-start.1) | collective-permute-done | bytes 131104 | tf_op jit(solution)/shard_map/ppermute | solution.py:20
  18.5 3.4 collective-permute-start.3
  22.0 1.4 collective-permute-start.2
  24.8 4.4 collective-permute-done.2
  29.3 2.0 fusion.49
  31.3 1.9 collective-permute-start.4
  33.2 2.4 collective-permute-start.5
  35.7 4.7 %collective-permute-done.5 = f32[16,1,16,128]{3,2,1,0:T(8,128)S(1)} collective-permute-done((f32[16,1,16,128]{3,2,1,0:T(8,128)S(1)}, f32[16,1,16,128]{3,2,1,0:T(8,128)S(1)}, u32[]{:S(2)}, u32[]{:S(2)}) %collective-permute-start.5) | collective-permute-done | bytes 131104 | tf_op jit(solution)/shard_map/ppermute | solution.py:20
  40.7 1.5 collective-permute-start.7
  42.2 1.3 collective-permute-start.6
  43.5 0.8 fusion.62
  44.9 4.3 collective-permute-done.6
  49.4 2.0 fusion.40
  51.4 1.9 collective-permute-start.8
  53.4 2.4 collective-permute-start.9
  55.9 4.7 collective-permute-done.9
  60.8 1.5 collective-permute-start.11
  62.3 1.4 collective-permute-start.10
  65.1 4.4 collective-permute-done.10
  69.6 2.8 fusion.31
  72.5 10.0 %copy.356 = f32[16,16,16,128]{0,3,2,1:T(8,128)} copy(f32[16,16,16,128]{3,2,1,0:T(8,128)} %fusion.31) | data formatting | bytes 4194304 | tf_op jit(solution)/shard_map/sub | solution.py:80
  82.5 9.4 %reduce_sum.9 = f32[16,4,4,32]{0,3,2,1:T(8,128)S(1)} reduce(f32[16,4,4,4,4,32,4]{0,6,5,4,3,2,1:T(4,128)} %bitcast.22, f32[]{:T(128)} %constant.11.clone.1), dimensions={2,4,6}, to_apply=%region_0.0 | reduce | flops 516096 | bytes 2129924 | tf_op jit(solution)/shard_map/reduce_sum | solution.py:49
  91.9 4.5 scatter_custom_fusion
  96.4 107.3 %all-reduce.15.cloned.1.call-done = f32[16,8192]{0,1:T(8,128)} async-done(((f32[16,8192]{0,1:T(8,128)}), f32[16,8192]{0,1:T(8,128)}) %all-reduce.15.cloned.1.call-update) | async-done | bytes 524304 | tf_op jit(solution)/shard_map/psum | solution.py:82
  203.7 3.5 copy.358
  208.1 91.3 %all-reduce.17.cloned.1.call-done = f32[16,64,128]{2,0,1:T(8,128)} async-done(((f32[16,64,128]{2,0,1:T(8,128)}), f32[16,64,128]{2,0,1:T(8,128)}) %all-reduce.17.cloned.1.call-update) | async-done | bytes 524304 | tf_op jit(solution)/shard_map/psum | solution.py:82
  299.4 57.4 %all-gather.2.cloned.1.call-done = f32[64,128,128]{2,1,0:T(8,128)} async-done(((f32[32,128,128]{2,1,0:T(8,128)}), f32[64,128,128]{2,1,0:T(8,128)}) %all-gather.2.cloned.1.call-update) | async-done | bytes 4194320 | tf_op jit(solution)/shard_map/all_gather | solution.py:83
  356.8 8.6 %convolution_bitcast_fusion.1 = f32[16,64,128]{2,0,1:T(8,128)S(1)} fusion(f32[16,64,128]{2,0,1:T(8,128)} %all-reduce.17.cloned.1.call-done, f32[64,128,128]{2,1,0:T(8,128)} %all-gather.2.cloned.1.call-done), kind=kOutput, calls=%fused_computation.105 | convolution fusion | flops 201326592 | bytes 5242880 | tf_op jit(solution)/shard_map/kbj,bij->kbi/dot_general | solution.py:70
  365.5 3.8 convolution_bitcast_fusion
  369.3 2.6 copy.384
  371.9 3.2 gather_fusion
  375.2 3.9 broadcast_in_dim.21
  379.1 5.7 %copy-done = f32[16,4,4,4,4,32,4]{0,6,5,4,3,2,1:T(4,128)} copy-done((f32[16,4,4,4,4,32,4]{0,6,5,4,3,2,1:T(4,128)}, f32[16,4,4,4,4,32,4]{0,6,5,4,3,2,1:T(4,128)S(1)}, u32[]{:S(2)}) %copy-start) | copy-done | bytes 2097176
  384.9 1.2 fusion.54
  386.0 1.5 copy.362
  387.6 2.6 collective-permute-start.12
  390.5 1.9 collective-permute-start.13
  392.5 11.0 %copy.373 = f32[16,16,16,128]{3,2,1,0:T(8,128)} copy(f32[16,16,16,128]{0,3,2,1:T(8,128)} %bitcast.21) | data formatting | bytes 4194304 | tf_op jit(solution)/shard_map/reshape | solution.py:62
  403.5 1.9 pad_maximum_fusion.56
  405.4 2.5 collective-permute-start.15
  407.9 1.3 collective-permute-start.14
  409.2 0.8 fusion.59
  410.0 2.0 collective-permute-done.15
  412.2 4.0 collective-permute-done.14
  416.3 2.0 fusion.24
  418.4 2.9 collective-permute-start.16
  421.3 1.9 collective-permute-start.17
  423.8 4.7 %collective-permute-done.17 = f32[16,1,16,128]{3,2,1,0:T(8,128)S(1)} collective-permute-done((f32[16,1,16,128]{3,2,1,0:T(8,128)S(1)}, f32[16,1,16,128]{3,2,1,0:T(8,128)S(1)}, u32[]{:S(2)}, u32[]{:S(2)}) %collective-permute-start.17) | collective-permute-done | bytes 131104 | tf_op jit(solution)/shard_map/ppermute | solution.py:20
  428.7 1.8 collective-permute-start.19
  430.5 1.6 collective-permute-start.18
  432.2 0.8 fusion.57
  433.3 4.4 collective-permute-done.18
  437.8 2.0 fusion.15
  439.9 1.9 collective-permute-start.20
  441.8 2.4 collective-permute-start.21
  444.3 4.7 %collective-permute-done.21 = f32[16,1,16,128]{3,2,1,0:T(8,128)S(1)} collective-permute-done((f32[16,1,16,128]{3,2,1,0:T(8,128)S(1)}, f32[16,1,16,128]{3,2,1,0:T(8,128)S(1)}, u32[]{:S(2)}, u32[]{:S(2)}) %collective-permute-start.21) | collective-permute-done | bytes 131104 | tf_op jit(solution)/shard_map/ppermute | solution.py:20
  449.2 1.5 collective-permute-start.23
  450.7 1.3 collective-permute-start.22
  452.0 0.8 fusion.55
  453.5 4.3 collective-permute-done.22
  457.9 3.0 fusion.6
  (75 shorter events, 9.6 us)
Async XLA Ops:
  6.5 197.2 %all-reduce.15.cloned.1.call-start = ((), (), s32[]{:S(2)}) async-start(), calls=%async_computation | async-start | bytes 8388608 | tf_op jit(solution)/shard_map/psum | solution.py:82
  8.4 5.2 %collective-permute-start = (f32[16,1,16,128]{3,2,1,0:T(8,128)S(1)}, f32[16,1,16,128]{3,2,1,0:T(8,128)S(1)}, u32[]{:S(2)}, u32[]{:S(2)}) collective-permute-start(f32[16,1,16,128]{3,2,1,0:T(8,128)S(1)} %get-tuple-element.40), channel_id=1, source_target_pairs={{2,0},{4,2},{6,4},{8,6},{10,8},{12,10},{14,12},{16,14},{18,16},{20... | collective-permute-start | bytes 393224 | tf_op jit(solution)/shard_map/ppermute | solution.py:22
  11.1 7.2 %collective-permute-start.1 = (f32[16,1,16,128]{3,2,1,0:T(8,128)S(1)}, f32[16,1,16,128]{3,2,1,0:T(8,128)S(1)}, u32[]{:S(2)}, u32[]{:S(2)}) collective-permute-start(f32[16,1,16,128]{3,2,1,0:T(8,128)S(1)} %get-tuple-element.39), channel_id=1, source_target_pairs={{0,2},{2,4},{4,6},{6,8},{8,10},{10,12},{12,14},{14,16},{16,18},{18... | collective-permute-start | bytes 393224 | tf_op jit(solution)/shard_map/ppermute | solution.py:20
  18.5 6.1 %collective-permute-start.3 = (f32[16,18,1,128]{3,0,2,1:T(8,128)S(1)}, f32[16,18,1,128]{3,0,2,1:T(8,128)S(1)}, u32[]{:S(2)}, u32[]{:S(2)}) collective-permute-start(f32[16,18,1,128]{3,0,2,1:T(8,128)S(1)} %copy.346), channel_id=1, source_target_pairs={{0,1},{2,3},{4,5},{6,7},{8,9},{10,11},{12,13},{14,15},{16,17},{18,... | collective-permute-start | bytes 442376 | tf_op jit(solution)/shard_map/ppermute | solution.py:20
  22.0 7.3 %copy-start.1 = (f32[16,16,16,128]{3,2,1,0:T(8,128)S(1)}, f32[16,16,16,128]{3,2,1,0:T(8,128)}, u32[]{:S(2)}) copy-start(f32[16,16,16,128]{3,2,1,0:T(8,128)} %param.3) | copy-start | bytes 6291460
  22.0 7.2 %collective-permute-start.2 = (f32[16,18,1,128]{3,0,2,1:T(8,128)S(1)}, f32[16,18,1,128]{3,0,2,1:T(8,128)S(1)}, u32[]{:S(2)}, u32[]{:S(2)}) collective-permute-start(f32[16,18,1,128]{3,0,2,1:T(8,128)S(1)} %copy.344), channel_id=1, source_target_pairs={{1,0},{3,2},{5,4},{7,6},{9,8},{11,10},{13,12},{15,14},{17,16},{19,... | collective-permute-start | bytes 442376 | tf_op jit(solution)/shard_map/ppermute | solution.py:22
  31.3 4.4 collective-permute-start.4
  33.2 7.2 %collective-permute-start.5 = (f32[16,1,16,128]{3,2,1,0:T(8,128)S(1)}, f32[16,1,16,128]{3,2,1,0:T(8,128)S(1)}, u32[]{:S(2)}, u32[]{:S(2)}) collective-permute-start(f32[16,1,16,128]{3,2,1,0:T(8,128)S(1)} %get-tuple-element.35), channel_id=1, source_target_pairs={{0,2},{2,4},{4,6},{6,8},{8,10},{10,12},{12,14},{14,16},{16,18},{18... | collective-permute-start | bytes 393224 | tf_op jit(solution)/shard_map/ppermute | solution.py:20
  40.7 4.1 collective-permute-start.7
  42.2 7.0 %collective-permute-start.6 = (f32[16,18,1,128]{3,0,2,1:T(8,128)S(1)}, f32[16,18,1,128]{3,0,2,1:T(8,128)S(1)}, u32[]{:S(2)}, u32[]{:S(2)}) collective-permute-start(f32[16,18,1,128]{3,0,2,1:T(8,128)S(1)} %copy.348), channel_id=1, source_target_pairs={{1,0},{3,2},{5,4},{7,6},{9,8},{11,10},{13,12},{15,14},{17,16},{19,... | collective-permute-start | bytes 442376 | tf_op jit(solution)/shard_map/ppermute | solution.py:22
  49.4 6.4 %copy-start.6 = (s32[4,4,32]{2,1,0:T(4,128)S(1)}, s32[4,4,32]{2,1,0:T(4,128)}, u32[]{:S(2)}) copy-start(s32[4,4,32]{2,1,0:T(4,128)} %param.4) | copy-start | bytes 6148
  51.4 4.4 collective-permute-start.8
  53.4 7.2 %collective-permute-start.9 = (f32[16,1,16,128]{3,2,1,0:T(8,128)S(1)}, f32[16,1,16,128]{3,2,1,0:T(8,128)S(1)}, u32[]{:S(2)}, u32[]{:S(2)}) collective-permute-start(f32[16,1,16,128]{3,2,1,0:T(8,128)S(1)} %get-tuple-element.31), channel_id=1, source_target_pairs={{0,2},{2,4},{4,6},{6,8},{8,10},{10,12},{12,14},{14,16},{16,18},{18... | collective-permute-start | bytes 393224 | tf_op jit(solution)/shard_map/ppermute | solution.py:20
  60.8 4.1 collective-permute-start.11
  62.3 7.3 %copy-start.2 = (f32[16,16,16,128]{3,2,1,0:T(8,128)S(1)}, f32[16,16,16,128]{3,2,1,0:T(8,128)}, u32[]{:S(2)}) copy-start(f32[16,16,16,128]{3,2,1,0:T(8,128)} %param.3) | copy-start | bytes 6291460
  62.3 7.2 %collective-permute-start.10 = (f32[16,18,1,128]{3,0,2,1:T(8,128)S(1)}, f32[16,18,1,128]{3,0,2,1:T(8,128)S(1)}, u32[]{:S(2)}, u32[]{:S(2)}) collective-permute-start(f32[16,18,1,128]{3,0,2,1:T(8,128)S(1)} %copy.352), channel_id=1, source_target_pairs={{1,0},{3,2},{5,4},{7,6},{9,8},{11,10},{13,12},{15,14},{17,16},{19,... | collective-permute-start | bytes 442376 | tf_op jit(solution)/shard_map/ppermute | solution.py:22
  96.4 203.1 %all-reduce.17.cloned.1.call-start = ((), (), s32[]{:S(2)}) async-start(), calls=%async_computation.1 | async-start | bytes 1048576 | tf_op jit(solution)/shard_map/psum | solution.py:82
  207.2 149.6 %all-gather.2.cloned.1.call-start = ((), (), s32[]{:S(2)}) async-start(), calls=%async_computation.2 | async-start | bytes 6291456 | tf_op jit(solution)/shard_map/all_gather | solution.py:83
  356.8 8.6 %copy-start.5 = (f32[64,128,128]{2,1,0:T(8,128)S(1)}, f32[64,128,128]{2,1,0:T(8,128)}, u32[]{:S(2)}) copy-start(f32[64,128,128]{2,1,0:T(8,128)} %all-gather.2.cloned.1.call-done) | copy-start | bytes 12582916
  379.1 5.8 %copy-start = (f32[16,4,4,4,4,32,4]{0,6,5,4,3,2,1:T(4,128)}, f32[16,4,4,4,4,32,4]{0,6,5,4,3,2,1:T(4,128)S(1)}, u32[]{:S(2)}) copy-start(f32[16,4,4,4,4,32,4]{0,6,5,4,3,2,1:T(4,128)S(1)} %broadcast_in_dim.21) | copy-start | bytes 6291460
  387.6 15.9 %collective-permute-start.12 = (f32[16,1,16,128]{3,2,1,0:T(8,128)S(1)}, f32[16,1,16,128]{3,2,1,0:T(8,128)S(1)}, u32[]{:S(2)}, u32[]{:S(2)}) collective-permute-start(f32[16,1,16,128]{3,2,1,0:T(8,128)S(1)} %copy.362), channel_id=1, source_target_pairs={{2,0},{4,2},{6,4},{8,6},{10,8},{12,10},{14,12},{16,14},{18,16},{20... | collective-permute-start | bytes 393224 | tf_op jit(solution)/shard_map/ppermute | solution.py:22
  390.5 12.9 %collective-permute-start.13 = (f32[16,1,16,128]{3,2,1,0:T(8,128)S(1)}, f32[16,1,16,128]{3,2,1,0:T(8,128)S(1)}, u32[]{:S(2)}, u32[]{:S(2)}) collective-permute-start(f32[16,1,16,128]{3,2,1,0:T(8,128)S(1)} %copy.364), channel_id=1, source_target_pairs={{0,2},{2,4},{4,6},{6,8},{8,10},{10,12},{12,14},{14,16},{16,18},{18... | collective-permute-start | bytes 393224 | tf_op jit(solution)/shard_map/ppermute | solution.py:20
  403.5 5.8 %copy-start.4 = (f32[16,16,16,128]{3,2,1,0:T(8,128)S(1)}, f32[16,16,16,128]{3,2,1,0:T(8,128)}, u32[]{:S(2)}) copy-start(f32[16,16,16,128]{3,2,1,0:T(8,128)} %copy.373) | copy-start | bytes 6291460
  405.4 6.6 %collective-permute-start.15 = (f32[16,18,1,128]{3,0,2,1:T(8,128)S(1)}, f32[16,18,1,128]{3,0,2,1:T(8,128)S(1)}, u32[]{:S(2)}, u32[]{:S(2)}) collective-permute-start(f32[16,18,1,128]{3,0,2,1:T(8,128)S(1)} %copy.369), channel_id=1, source_target_pairs={{0,1},{2,3},{4,5},{6,7},{8,9},{10,11},{12,13},{14,15},{16,17},{18,... | collective-permute-start | bytes 442376 | tf_op jit(solution)/shard_map/ppermute | solution.py:20
  407.9 8.2 %collective-permute-start.14 = (f32[16,18,1,128]{3,0,2,1:T(8,128)S(1)}, f32[16,18,1,128]{3,0,2,1:T(8,128)S(1)}, u32[]{:S(2)}, u32[]{:S(2)}) collective-permute-start(f32[16,18,1,128]{3,0,2,1:T(8,128)S(1)} %copy.367), channel_id=1, source_target_pairs={{1,0},{3,2},{5,4},{7,6},{9,8},{11,10},{13,12},{15,14},{17,16},{19,... | collective-permute-start | bytes 442376 | tf_op jit(solution)/shard_map/ppermute | solution.py:22
  418.4 5.5 %collective-permute-start.16 = (f32[16,1,16,128]{3,2,1,0:T(8,128)S(1)}, f32[16,1,16,128]{3,2,1,0:T(8,128)S(1)}, u32[]{:S(2)}, u32[]{:S(2)}) collective-permute-start(f32[16,1,16,128]{3,2,1,0:T(8,128)S(1)} %get-tuple-element.26), channel_id=1, source_target_pairs={{2,0},{4,2},{6,4},{8,6},{10,8},{12,10},{14,12},{16,14},{18,16},{20... | collective-permute-start | bytes 393224 | tf_op jit(solution)/shard_map/ppermute | solution.py:22
  421.3 7.2 %collective-permute-start.17 = (f32[16,1,16,128]{3,2,1,0:T(8,128)S(1)}, f32[16,1,16,128]{3,2,1,0:T(8,128)S(1)}, u32[]{:S(2)}, u32[]{:S(2)}) collective-permute-start(f32[16,1,16,128]{3,2,1,0:T(8,128)S(1)} %get-tuple-element.25), channel_id=1, source_target_pairs={{0,2},{2,4},{4,6},{6,8},{8,10},{10,12},{12,14},{14,16},{16,18},{18... | collective-permute-start | bytes 393224 | tf_op jit(solution)/shard_map/ppermute | solution.py:20
  428.7 4.4 collective-permute-start.19
  430.5 7.3 %copy-start.3 = (f32[16,16,16,128]{3,2,1,0:T(8,128)S(1)}, f32[16,16,16,128]{3,2,1,0:T(8,128)}, u32[]{:S(2)}) copy-start(f32[16,16,16,128]{3,2,1,0:T(8,128)} %param.3) | copy-start | bytes 6291460
  430.5 7.2 %collective-permute-start.18 = (f32[16,18,1,128]{3,0,2,1:T(8,128)S(1)}, f32[16,18,1,128]{3,0,2,1:T(8,128)S(1)}, u32[]{:S(2)}, u32[]{:S(2)}) collective-permute-start(f32[16,18,1,128]{3,0,2,1:T(8,128)S(1)} %copy.374), channel_id=1, source_target_pairs={{1,0},{3,2},{5,4},{7,6},{9,8},{11,10},{13,12},{15,14},{17,16},{19,... | collective-permute-start | bytes 442376 | tf_op jit(solution)/shard_map/ppermute | solution.py:22
  439.9 4.4 collective-permute-start.20
  441.8 7.2 %collective-permute-start.21 = (f32[16,1,16,128]{3,2,1,0:T(8,128)S(1)}, f32[16,1,16,128]{3,2,1,0:T(8,128)S(1)}, u32[]{:S(2)}, u32[]{:S(2)}) collective-permute-start(f32[16,1,16,128]{3,2,1,0:T(8,128)S(1)} %get-tuple-element.21), channel_id=1, source_target_pairs={{0,2},{2,4},{4,6},{6,8},{8,10},{10,12},{12,14},{14,16},{16,18},{18... | collective-permute-start | bytes 393224 | tf_op jit(solution)/shard_map/ppermute | solution.py:20
  449.2 4.1 collective-permute-start.23
  450.7 7.0 %collective-permute-start.22 = (f32[16,18,1,128]{3,0,2,1:T(8,128)S(1)}, f32[16,18,1,128]{3,0,2,1:T(8,128)S(1)}, u32[]{:S(2)}, u32[]{:S(2)}) collective-permute-start(f32[16,18,1,128]{3,0,2,1:T(8,128)S(1)} %copy.378), channel_id=1, source_target_pairs={{1,0},{3,2},{5,4},{7,6},{9,8},{11,10},{13,12},{15,14},{17,16},{19,... | collective-permute-start | bytes 442376 | tf_op jit(solution)/shard_map/ppermute | solution.py:22
Sparse Core Ops, SparseCore 0:
  96.5 107.1 all-reduce.14
  207.4 92.0 all-reduce.16
  301.0 55.8 all-gather.1
